TPU v7x, 32 devices: a whole 2x2x4 slice. The times are simulated.
32 devices in a mesh: img: 8 (over y, x, core), head: 4 (over z).
Axes of the slice: x: 2, y: 2, z: 4, core: 2. Of those that a mesh axis runs over, the one named last changes fastest.
Arguments:
- latents: bfloat16 [192, 64, 1024], P('img'), may hold values from -6 to 6
- media: bfloat16 [192, 256, 1024], P('img'), may hold values from -6 to 6
- valid_counts: int32 [192], P('img'), may hold values from 160 to 256, as said below
- w_query: bfloat16 [1024, 512], P(None, 'head'), may hold values from -0.1875 to 0.1875
- w_key: bfloat16 [1024, 512], P(None, 'head'), may hold values from -0.1875 to 0.1875
- w_value: bfloat16 [1024, 512], P(None, 'head'), may hold values from -0.1875 to 0.1875
- w_out: bfloat16 [1024, 512], P(None, 'head'), may hold values from -2 to 2
- w_up: bfloat16 [1024, 4096], P(None, 'head'), may hold values from -0.1875 to 0.1875
- w_down: bfloat16 [1024, 4096], P(None, 'head'), may hold values from -0.09375 to 0.09375
- norm_gains: float32 [3, 1024], replicated, may hold values from 0.5 to 1.5
- norm_biases: float32 [3, 1024], replicated, may hold values from -1.8 to 1.8
- cotangent: bfloat16 [192, 64, 1024], P('img'), may hold values from -6 to 6
Outputs:
- latents_out: bfloat16 [192, 64, 1024], P('img')
- latents_grad: bfloat16 [192, 64, 1024], P('img', 'head')
- media_grad: bfloat16 [192, 256, 1024], P('img', 'head')
- w_query_grad: float32 [1024, 512], P('img', 'head')
- w_key_grad: float32 [1024, 512], P('img', 'head')
- w_value_grad: float32 [1024, 512], P('img', 'head')
- w_out_grad: float32 [1024, 512], P('img', 'head')
- w_up_grad: float32 [1024, 4096], P('img', 'head')
- w_down_grad: float32 [1024, 4096], P('img', 'head')
- norm_gains_grad: float32 [3, 1024], P(None, ('img', 'head'))
- norm_biases_grad: float32 [3, 1024], P(None, ('img', 'head'))
Inputs may be any that keep to these rules, and one draw needn't show every extreme that they name: An image's valid patch keys are its first valid_counts patches; some image has exactly 256 and some exactly 160.
All inputs are finite; a program needn't handle non-finite values.
Results may differ from a plain program's by a relative error of at most 0.018.
Values may be sent and summed in bfloat16 or wider, within the bound.
No kernel may reach another device: no remote copies, remote signals or barrier semaphores. Data moves between devices by JAX's collectives and lax.ppermute only.
A program may use at most 192 MiB of HBM per device.

v0:
```python
import jax
import jax.numpy as jnp
from jax import lax
from jax.sharding import PartitionSpec as P

HEAD_DIM = 64
epsilon = 1e-05


def layer_norm(values, gain_row, bias_row):
    center = jnp.mean(values, axis=-1, keepdims=True)
    centered = values - center
    spread = jnp.mean(centered * centered, axis=-1, keepdims=True)
    return centered * lax.rsqrt(spread + epsilon) * gain_row + bias_row


def exact_gelu(values):
    return jax.nn.gelu(values, approximate=False)


def rows_share(values, member, count):
    return lax.dynamic_slice_in_dim(values, member * count, count, 1)


def body(
    latents,
    media,
    valid_counts,
    w_query,
    w_key,
    w_value,
    w_out,
    w_up,
    w_down,
    norm_gains,
    norm_biases,
    cotangent,
):
    groups = lax.axis_size("head")
    member = lax.axis_index("head")
    images, patches, model_width = media.shape
    latent_rows = latents.shape[1]
    share_rows = latent_rows // groups
    local_width = w_query.shape[1]
    local_heads = local_width // HEAD_DIM
    score_scale = HEAD_DIM ** (-0.5)
    latent_in = latents.astype(jnp.float32)
    media_in = media.astype(jnp.float32)
    media_normed = layer_norm(media_in, norm_gains[0], norm_biases[0]).astype(jnp.bfloat16)
    latent_normed = layer_norm(latent_in, norm_gains[1], norm_biases[1]).astype(jnp.bfloat16)
    joint_weight = jnp.concatenate([w_query, w_key, w_value], axis=1)
    media_kv = jnp.einsum(
        "ipd,de->ipe",
        media_normed,
        joint_weight[:, local_width:],
        preferred_element_type=jnp.float32,
    ).astype(jnp.bfloat16)
    latent_qkv = jnp.einsum(
        "ild,de->ile", latent_normed, joint_weight, preferred_element_type=jnp.float32
    ).astype(jnp.bfloat16)
    queries = latent_qkv[..., :local_width].reshape(images, latent_rows, local_heads, HEAD_DIM)
    key_rows = jnp.concatenate(
        [media_kv[..., :local_width], latent_qkv[..., local_width : 2 * local_width]], axis=1
    )
    key_rows = key_rows.reshape(images, patches + latent_rows, local_heads, HEAD_DIM)
    value_rows = jnp.concatenate(
        [media_kv[..., local_width:], latent_qkv[..., 2 * local_width :]], axis=1
    )
    value_rows = value_rows.reshape(images, patches + latent_rows, local_heads, HEAD_DIM)
    positions = lax.iota(jnp.int32, patches + latent_rows)
    allowed = (positions[None, :] < valid_counts[:, None]) | (positions[None, :] >= patches)
    scores = (
        jnp.einsum("ilhe,ikhe->ihlk", queries, key_rows, preferred_element_type=jnp.float32)
        * score_scale
    )
    scores = jnp.where(allowed[:, None, None, :], scores, -1e30)
    attention = jax.nn.softmax(scores, axis=-1)
    attention_low = attention.astype(jnp.bfloat16)
    attended = jnp.einsum(
        "ihlk,ikhe->ilhe", attention_low, value_rows, preferred_element_type=jnp.float32
    )
    attended = attended.astype(jnp.bfloat16).reshape(images, latent_rows, local_width)
    attn_part = jnp.einsum("ile,de->ild", attended, w_out, preferred_element_type=jnp.float32)
    residual = latent_in + lax.psum(attn_part.astype(jnp.bfloat16), "head").astype(jnp.float32)
    ffn_low = layer_norm(residual, norm_gains[2], norm_biases[2]).astype(jnp.bfloat16)
    pre_act = jnp.einsum("ild,df->ilf", ffn_low, w_up, preferred_element_type=jnp.float32)
    hidden, gelu_puller = jax.vjp(exact_gelu, pre_act)
    hidden_low = hidden.astype(jnp.bfloat16)
    mlp_part = jnp.einsum("ilf,df->ild", hidden_low, w_down, preferred_element_type=jnp.float32)
    latents_out = (
        residual + lax.psum(mlp_part.astype(jnp.bfloat16), "head").astype(jnp.float32)
    ).astype(jnp.bfloat16)
    upstream = cotangent.astype(jnp.float32)
    grad_down = jnp.einsum("ild,ilf->df", cotangent, hidden_low, preferred_element_type=jnp.float32)
    grad_hidden = jnp.einsum("ild,df->ilf", cotangent, w_down, preferred_element_type=jnp.float32)
    grad_pre = gelu_puller(grad_hidden)[0].astype(jnp.bfloat16)
    grad_up = jnp.einsum("ild,ilf->df", ffn_low, grad_pre, preferred_element_type=jnp.float32)
    grad_ffn_part = jnp.einsum("ilf,df->ild", grad_pre, w_up, preferred_element_type=jnp.float32)
    grad_ffn = lax.psum(grad_ffn_part.astype(jnp.bfloat16), "head").astype(jnp.float32)
    norm_puller = jax.vjp(layer_norm, residual, norm_gains[2], norm_biases[2])[1]
    grad_from_norm, gain_ffn, bias_ffn = norm_puller(grad_ffn)
    grad_residual = upstream + grad_from_norm
    grad_low = grad_residual.astype(jnp.bfloat16)
    grad_residual_share = rows_share(grad_residual, member, share_rows)
    gain_ffn = gain_ffn / groups
    bias_ffn = bias_ffn / groups
    grad_wout = jnp.einsum("ild,ile->de", grad_low, attended, preferred_element_type=jnp.float32)
    grad_attended = jnp.einsum("ild,de->ile", grad_low, w_out, preferred_element_type=jnp.float32)
    grad_attended = grad_attended.astype(jnp.bfloat16).reshape(
        images, latent_rows, local_heads, HEAD_DIM
    )
    grad_values = jnp.einsum(
        "ihlk,ilhe->ikhe", attention_low, grad_attended, preferred_element_type=jnp.float32
    )
    grad_attention = jnp.einsum(
        "ilhe,ikhe->ihlk", grad_attended, value_rows, preferred_element_type=jnp.float32
    )
    row_total = jnp.sum(attention * grad_attention, axis=-1, keepdims=True)
    grad_scores = (attention * (grad_attention - row_total)).astype(jnp.bfloat16)
    grad_queries = (
        jnp.einsum("ihlk,ikhe->ilhe", grad_scores, key_rows, preferred_element_type=jnp.float32)
        * score_scale
    )
    grad_keys = (
        jnp.einsum("ihlk,ilhe->ikhe", grad_scores, queries, preferred_element_type=jnp.float32)
        * score_scale
    )
    grad_queries = grad_queries.astype(jnp.bfloat16).reshape(images, latent_rows, local_width)
    grad_keys = grad_keys.astype(jnp.bfloat16).reshape(images, patches + latent_rows, local_width)
    grad_values = grad_values.astype(jnp.bfloat16).reshape(
        images, patches + latent_rows, local_width
    )
    media_grad_kv = jnp.concatenate([grad_keys[:, :patches], grad_values[:, :patches]], axis=2)
    latent_grad_qkv = jnp.concatenate(
        [grad_queries, grad_keys[:, patches:], grad_values[:, patches:]], axis=2
    )
    media_weight_grad = jnp.einsum(
        "ipd,ipe->de", media_normed, media_grad_kv, preferred_element_type=jnp.float32
    )
    latent_weight_grad = jnp.einsum(
        "ild,ile->de", latent_normed, latent_grad_qkv, preferred_element_type=jnp.float32
    )
    grad_wq = latent_weight_grad[:, :local_width]
    grad_wk = (
        media_weight_grad[:, :local_width] + latent_weight_grad[:, local_width : 2 * local_width]
    )
    grad_wv = media_weight_grad[:, local_width:] + latent_weight_grad[:, 2 * local_width :]
    grads_out = (
        lax.psum_scatter(grad_wq, "img", scatter_dimension=0, tiled=True),
        lax.psum_scatter(grad_wk, "img", scatter_dimension=0, tiled=True),
        lax.psum_scatter(grad_wv, "img", scatter_dimension=0, tiled=True),
        lax.psum_scatter(grad_wout, "img", scatter_dimension=0, tiled=True),
        lax.psum_scatter(grad_up, "img", scatter_dimension=0, tiled=True),
        lax.psum_scatter(grad_down, "img", scatter_dimension=0, tiled=True),
    )
    media_part = jnp.einsum(
        "ipe,de->ipd",
        media_grad_kv,
        joint_weight[:, local_width:],
        preferred_element_type=jnp.float32,
    )
    latent_part = jnp.einsum(
        "ile,de->ild", latent_grad_qkv, joint_weight, preferred_element_type=jnp.float32
    )
    media_share, latent_share = (
        lax.psum_scatter(
            media_part.astype(jnp.bfloat16), "head", scatter_dimension=1, tiled=True
        ).astype(jnp.float32),
        lax.psum_scatter(
            latent_part.astype(jnp.bfloat16), "head", scatter_dimension=1, tiled=True
        ).astype(jnp.float32),
    )
    media_rows = patches // groups
    media_puller = jax.vjp(
        layer_norm, rows_share(media_in, member, media_rows), norm_gains[0], norm_biases[0]
    )[1]
    grad_media_in, gain_media, bias_media = media_puller(media_share)
    latent_puller = jax.vjp(
        layer_norm, rows_share(latent_in, member, share_rows), norm_gains[1], norm_biases[1]
    )[1]
    grad_latent_norm, gain_latent, bias_latent = latent_puller(latent_share)
    latents_grad = (grad_residual_share + grad_latent_norm).astype(jnp.bfloat16)
    media_grad = grad_media_in.astype(jnp.bfloat16)
    gain_terms = jnp.stack([gain_media, gain_latent, gain_ffn])
    bias_terms = jnp.stack([bias_media, bias_latent, bias_ffn])
    gain_total, bias_total = (
        lax.psum_scatter(gain_terms, ("img", "head"), scatter_dimension=1, tiled=True),
        lax.psum_scatter(bias_terms, ("img", "head"), scatter_dimension=1, tiled=True),
    )
    return (
        latents_out,
        latents_grad,
        media_grad,
        grads_out[0],
        grads_out[1],
        grads_out[2],
        grads_out[3],
        grads_out[4],
        grads_out[5],
        gain_total,
        bias_total,
    )


def solution(mesh):
    return jax.shard_map(
        body,
        mesh=mesh,
        in_specs=(
            P("img", None, None),
            P("img", None, None),
            P("img"),
            P(None, "head"),
            P(None, "head"),
            P(None, "head"),
            P(None, "head"),
            P(None, "head"),
            P(None, "head"),
            P(),
            P(),
            P("img", None, None),
        ),
        out_specs=(
            P("img", None, None),
            P("img", "head", None),
            P("img", "head", None),
            P("img", "head"),
            P("img", "head"),
            P("img", "head"),
            P("img", "head"),
            P("img", "head"),
            P("img", "head"),
            P(None, ("img", "head")),
            P(None, ("img", "head")),
        ),
        check_vma=False,
    )
```

profile of v0, /device:TPU:0, one launch (start us, length us, event | category | flops | bytes accessed | tf_op | source)
XLA Modules:
  0.0 1304.9 jit_solution(8463983802196653508)
XLA Ops:
  7.8 2.4 convert_reduce_fusion.5
  10.2 2.9 multiply_reduce_fusion.3
  13.8 6.3 convert_reduce_fusion
  20.2 8.3 multiply_reduce_fusion
  29.1 2.2 fusion.41
  32.9 8.5 fusion.23
  42.6 2.2 pad_maximum_fusion.3
  44.9 4.2 copy.55
  49.1 4.1 copy.56
  53.2 5.5 fusion.74
  58.7 4.1 convolution_convert_fusion.6
  62.8 2.7 convolution_convert_fusion.3
  65.9 123.6 %all-reduce.4.cloned.1.call-done = bf16[24,64,1024]{2,1,0:T(8,128)(2,1)} async-done(((bf16[24,64,1024]{2,1,0:T(8,128)(2,1)}), bf16[24,64,1024]{2,1,0:T(8,128)(2,1)}) %all-reduce.4.cloned.1.call-update) | async-done | bytes 3145744 | tf_op jit(solution)/shard_map/psum | solution.py:84
  189.5 3.9 fusion.18
  194.2 1.3 multiply_reduce_fusion.2
  195.6 5.7 convert_reduce_fusion.4
  201.3 14.4 %multiply_convert_fusion = (bf16[24,64,1024]{2,1,0:T(8,128)(2,1)S(1)}, f32[24,64,1024]{2,1,0:T(8,128)S(1)}) fusion(f32[24,64,1024]{2,1,0:T(8,128)S(1)} %get-tuple-element.86, u32[64,1024]{1,0:T(8,128)S(1)} %get-tuple-element.55, u32[64,1024]{1,0:T(8,128)S(1)} %get-tuple-element.54), kind=kLoop, calls=%fused_computation.35 | loop fusion | flops 106954752 | bytes 16252928 | tf_op jit(solution)/shard_map/convert_element_type | solution.py:88
  215.7 6.4 add_convert_fusion.4
  222.0 6.7 convolution_convert_fusion.1
  228.8 4.8 convolution_convert_fusion.2
  233.7 222.0 %all-reduce.6.cloned.1.call-done = (bf16[24,64,1024]{2,1,0:T(8,128)(2,1)}, bf16[24,64,1024]{2,1,0:T(8,128)(2,1)}) async-done(((bf16[24,64,1024]{2,1,0:T(8,128)(2,1)}, bf16[24,64,1024]{2,1,0:T(8,128)(2,1)}), (bf16[24,64,1024]{2,1,0:T(8,128)(2,1)}, bf16[24,64,1024]{2,1,0:T(8,128)(2,1)})) %all-reduce.6.cloned.1.call-update) | async-done | bytes 6291472 | tf_op jit(solution)/shard_map/psum | solution.py:91
  455.7 5.4 convert_reduce_fusion.2
  461.1 6.5 fusion.10
  467.7 4.2 add_add_fusion.2
  471.9 2.6 copy-done.5
  475.9 3.3 convolution_convert_fusion.5
  480.3 1.6 multiply_reduce_fusion.4
  484.5 2.1 multiply_convert_fusion.1
  487.4 1.3 slice.91
  489.1 4.7 convolution_convert_fusion.4
  493.9 1.6 slice.94
  495.6 2.7 slice.93
  498.2 1.8 copy.80
  500.0 1.9 copy.79
  502.0 8.5 convolution_convert_fusion
  510.6 8.4 convolution_bitcast_fusion
  519.0 5.2 convert_element_type.105
  524.3 14.3 %convert_element_type.106 = f32[24,256,1024]{2,1,0:T(8,128)} convert(bf16[24,256,1024]{2,1,0:T(8,128)(2,1)} %param.13) | non-fusion elementwise | flops 6291456 | bytes 37748736 | tf_op jit(solution)/shard_map/convert_element_type | solution.py:48
  538.6 1.6 dynamic-slice_reduce_fusion.1
  540.1 3.2 dynamic-slice_reduce_fusion
  543.4 10.0 reduce-scatter.15.cloned.1.call-done
  553.3 2.3 multiply_reduce_fusion.5
  555.6 2.5 fusion.36
  558.1 209.2 %reduce-scatter.17.cloned.1.call-done = bf16[24,64,1024]{2,1,0:T(8,128)(2,1)} async-done(((bf16[24,256,1024]{2,1,0:T(8,128)(2,1)}), bf16[24,64,1024]{2,1,0:T(8,128)(2,1)}) %reduce-scatter.17.cloned.1.call-update) | async-done | bytes 3145744 | tf_op jit(solution)/shard_map/reduce_scatter | solution.py:166
  767.3 6.1 multiply_reduce_fusion.1
  773.5 5.8 fusion.11
  781.9 10.5 convolution_bitcast_fusion.1
  792.5 6.3 fusion.47
  798.8 9.2 fusion.43
  808.1 4.1 fusion.42
  812.2 1.2 slice_add_fusion
  814.8 7.8 reduce-scatter.29.cloned.1.call-done
  822.7 2.0 copy.69
  824.7 3.3 add_convert_fusion.12
  828.1 6.1 add_convert_fusion.3
  834.2 126.4 %reduce-scatter.31.cloned.1.call-done = f32[32,3]{1,0:T(8,128)} async-done(((f32[1024,3]{1,0:T(8,128)}), f32[32,3]{1,0:T(8,128)}) %reduce-scatter.31.cloned.1.call-update) | async-done | bytes 400
  960.6 1.4 copy.74
  961.9 133.5 %reduce-scatter.33.cloned.1.call-done = f32[32,3]{1,0:T(8,128)} async-done(((f32[1024,3]{1,0:T(8,128)}), f32[32,3]{1,0:T(8,128)}) %reduce-scatter.33.cloned.1.call-update) | async-done | bytes 400
  1095.5 1.4 copy.76
  1096.9 49.8 %reduce-scatter.27.cloned.1.call-done = f32[128,1024]{1,0:T(8,128)} async-done(((f32[1024,1024]{1,0:T(8,128)}), f32[128,1024]{1,0:T(8,128)}) %reduce-scatter.27.cloned.1.call-update) | async-done | bytes 524304 | tf_op jit(solution)/shard_map/reduce_scatter | solution.py:153
  1146.6 37.8 %reduce-scatter.25.cloned.1.call-done = f32[128,128]{1,0:T(8,128)} async-done(((f32[1024,128]{1,0:T(8,128)}), f32[128,128]{1,0:T(8,128)}) %reduce-scatter.25.cloned.1.call-update) | async-done | bytes 65552 | tf_op jit(solution)/shard_map/reduce_scatter | solution.py:152
  1184.5 37.7 %reduce-scatter.23.cloned.1.call-done = f32[128,128]{1,0:T(8,128)} async-done(((f32[1024,128]{1,0:T(8,128)}), f32[128,128]{1,0:T(8,128)}) %reduce-scatter.23.cloned.1.call-update) | async-done | bytes 65552 | tf_op jit(solution)/shard_map/reduce_scatter | solution.py:151
  1222.1 37.8 %reduce-scatter.21.cloned.1.call-done = f32[128,128]{1,0:T(8,128)} async-done(((f32[1024,128]{1,0:T(8,128)}), f32[128,128]{1,0:T(8,128)}) %reduce-scatter.21.cloned.1.call-update) | async-done | bytes 65552 | tf_op jit(solution)/shard_map/reduce_scatter | solution.py:150
  1259.9 37.7 %reduce-scatter.19.cloned.1.call-done = f32[128,128]{1,0:T(8,128)} async-done(((f32[1024,128]{1,0:T(8,128)}), f32[128,128]{1,0:T(8,128)}) %reduce-scatter.19.cloned.1.call-update) | async-done | bytes 65552 | tf_op jit(solution)/shard_map/reduce_scatter | solution.py:149
  (179 shorter events, 16.3 us)
Async XLA Ops:
  7.2 188.4 %copy-start = (bf16[1024,1024]{1,0:T(8,128)(2,1)S(1)}, bf16[1024,1024]{1,0:T(8,128)(2,1)}, u32[]{:S(2)}) copy-start(bf16[1024,1024]{1,0:T(8,128)(2,1)} %param.19) | copy-start | bytes 6291460
  7.2 5.9 copy-start.48
  7.2 6.0 copy-start.49
  7.2 182.3 %all-reduce.4.cloned.1.call-start = ((), (), s32[]{:S(2)}) async-start(), calls=%async_computation.10 | async-start | bytes 6291456 | tf_op jit(solution)/shard_map/psum | solution.py:84
  10.2 18.9 %copy-start.43 = (f32[24,64]{1,0:T(8,128)}, f32[24,64]{1,0:T(8,128)S(1)}, u32[]{:S(2)}) copy-start(f32[24,64]{1,0:T(8,128)S(1)} %broadcast_multiply_fusion.4) | copy-start | bytes 18436
  13.1 16.0 %copy-start.47 = (f32[24,64]{1,0:T(8,128)}, f32[24,64]{1,0:T(8,128)S(1)}, u32[]{:S(2)}) copy-start(f32[24,64]{1,0:T(8,128)S(1)} %add_rsqrt_fusion.1) | copy-start | bytes 18436
  13.2 15.9 %copy-start.41 = (f32[1,1024]{1,0:T(1,128)}, f32[1,1024]{1,0:T(1,128)S(1)}, u32[]{:S(2)}) copy-start(f32[1,1024]{1,0:T(1,128)S(1)} %get-tuple-element.76) | copy-start | bytes 12292
  13.2 454.5 %copy-start.39 = (f32[1,1024]{1,0:T(1,128)}, f32[1,1024]{1,0:T(1,128)S(1)}, u32[]{:S(2)}) copy-start(f32[1,1024]{1,0:T(1,128)S(1)} %get-tuple-element.74) | copy-start | bytes 12292
  13.8 15.3 %copy-start.50 = (f32[1,1024]{1,0:T(1,128)}, f32[1,1024]{1,0:T(1,128)S(1)}, u32[]{:S(2)}) copy-start(f32[1,1024]{1,0:T(1,128)S(1)} %get-tuple-element.79) | copy-start | bytes 12292
  20.1 8.4 copy-start.37
  20.1 9.0 copy-start.2
  20.1 9.0 copy-start.29
  20.1 9.0 copy-start.31
  20.2 9.0 copy-start.57
  32.9 20.3 %copy-start.17 = (bf16[24,64,128]{1,2,0:T(8,128)(2,1)}, bf16[24,64,128]{1,2,0:T(8,128)(2,1)S(1)}, u32[]{:S(2)}) copy-start(bf16[24,64,128]{1,2,0:T(8,128)(2,1)S(1)} %copy.81) | copy-start | bytes 1179652
  44.9 8.3 copy-start.54
  44.9 8.3 copy-start.55
  65.6 130.0 %copy-start.53 = (f32[1,1024]{1,0:T(1,128)S(1)}, f32[1,1024]{1,0:T(1,128)}, u32[]{:S(2)}) copy-start(f32[1,1024]{1,0:T(1,128)} %get-tuple-element.77) | copy-start | bytes 12292
  65.6 390.1 %all-reduce.6.cloned.1.call-start = ((), (), s32[]{:S(2)}) async-start(), calls=%async_computation.21 | async-start | bytes 12582912 | tf_op jit(solution)/shard_map/psum | solution.py:91
  189.5 4.7 copy-start.6
  201.2 14.4 %copy-start.14 = (bf16[24,64,1024]{2,1,0:T(8,128)(2,1)S(1)}, bf16[24,64,1024]{2,1,0:T(8,128)(2,1)}, u32[]{:S(2)}) copy-start(bf16[24,64,1024]{2,1,0:T(8,128)(2,1)} %param.23) | copy-start | bytes 9437188
  201.3 14.4 %copy-start.56 = (bf16[1024,1024]{1,0:T(8,128)(2,1)S(1)}, bf16[1024,1024]{1,0:T(8,128)(2,1)}, u32[]{:S(2)}) copy-start(bf16[1024,1024]{1,0:T(8,128)(2,1)} %param.20) | copy-start | bytes 6291460
  215.6 13.1 %copy-start.19 = (bf16[24,64,1024]{2,1,0:T(8,128)(2,1)}, bf16[24,64,1024]{2,1,0:T(8,128)(2,1)S(1)}, u32[]{:S(2)}) copy-start(bf16[24,64,1024]{2,1,0:T(8,128)(2,1)S(1)} %get-tuple-element.62) | copy-start | bytes 9437188
  233.6 319.7 %reduce-scatter.15.cloned.1.call-start = ((), (), s32[]{:S(2)}) async-start(), calls=%async_computation.11 | async-start | bytes 3932160 | tf_op jit(solution)/shard_map/reduce_scatter | solution.py:169
  455.7 5.5 copy-start.9
  455.7 12.0 copy-start.16
  461.1 6.6 copy-start.4
  461.1 6.6 copy-start.7
  461.1 6.6 copy-start.15
  467.7 6.8 copy-start.25
  474.5 4.8 slice-start
  475.9 4.4 copy-start.21
  480.3 6.4 copy-start.20
  487.4 6.5 copy-start.26
  489.1 4.8 copy-start.28
  493.9 273.5 %reduce-scatter.17.cloned.1.call-start = ((), (), s32[]{:S(2)}) async-start(), calls=%async_computation.12 | async-start | bytes 15728640 | tf_op jit(solution)/shard_map/reduce_scatter | solution.py:166
  493.9 8.0 copy-start.30
  493.9 8.0 copy-start.32
  501.9 8.5 copy-start.13
  510.5 312.2 %reduce-scatter.29.cloned.1.call-start = ((), (), s32[]{:S(2)}) async-start(), calls=%async_computation.18 | async-start | bytes 4718592 | tf_op jit(solution)/shard_map/reduce_scatter | solution.py:154
  519.0 441.6 %reduce-scatter.31.cloned.1.call-start = ((), (), s32[]{:S(2)}) async-start(), calls=%async_computation.19 | async-start | bytes 540672
  538.6 14.7 %copy-start.42 = (f32[1,1024]{1,0:T(1,128)S(1)}, f32[1,1024]{1,0:T(1,128)}, u32[]{:S(2)}) copy-start(f32[1,1024]{1,0:T(1,128)} %copy-done.41) | copy-start | bytes 12292
  767.3 6.1 copy-start.8
  773.4 8.5 copy-start.40
  773.4 18.9 %copy-start.33 = (f32[24,64]{1,0:T(8,128)}, f32[24,64]{1,0:T(8,128)S(1)}, u32[]{:S(2)}) copy-start(f32[24,64]{1,0:T(8,128)S(1)} %get-tuple-element.80) | copy-start | bytes 18436
  773.4 18.9 %copy-start.35 = (f32[24,64]{1,0:T(8,128)}, f32[24,64]{1,0:T(8,128)S(1)}, u32[]{:S(2)}) copy-start(f32[24,64]{1,0:T(8,128)S(1)} %get-tuple-element.81) | copy-start | bytes 18436
  780.4 315.1 %reduce-scatter.33.cloned.1.call-start = ((), (), s32[]{:S(2)}) async-start(), calls=%async_computation.20 | async-start | bytes 540672
  781.6 365.1 %reduce-scatter.27.cloned.1.call-start = ((), (), s32[]{:S(2)}) async-start(), calls=%async_computation.17 | async-start | bytes 4718592 | tf_op jit(solution)/shard_map/reduce_scatter | solution.py:153
  792.4 6.4 copy-start.12
  792.4 6.4 copy-start.38
  792.4 6.4 copy-start.46
  792.4 6.4 copy-start.52
  792.4 392.0 %reduce-scatter.25.cloned.1.call-start = ((), (), s32[]{:S(2)}) async-start(), calls=%async_computation.16 | async-start | bytes 589824 | tf_op jit(solution)/shard_map/reduce_scatter | solution.py:152
  798.8 9.3 copy-start.27
  798.8 9.3 copy-start.44
  798.8 9.3 copy-start.51
  808.1 414.1 %reduce-scatter.23.cloned.1.call-start = ((), (), s32[]{:S(2)}) async-start(), calls=%async_computation.15 | async-start | bytes 589824 | tf_op jit(solution)/shard_map/reduce_scatter | solution.py:151
  812.2 12.5 copy-start.11
  812.2 15.8 %copy-start.45 = (f32[24,64]{1,0:T(8,128)S(1)}, f32[24,64]{1,0:T(8,128)}, u32[]{:S(2)}) copy-start(f32[24,64]{1,0:T(8,128)} %get-tuple-element.45) | copy-start | bytes 18436
  812.2 15.8 %copy-start.34 = (f32[24,64]{1,0:T(8,128)S(1)}, f32[24,64]{1,0:T(8,128)}, u32[]{:S(2)}) copy-start(f32[24,64]{1,0:T(8,128)} %copy-done.33) | copy-start | bytes 18436
  812.2 15.8 %copy-start.36 = (f32[24,64]{1,0:T(8,128)S(1)}, f32[24,64]{1,0:T(8,128)}, u32[]{:S(2)}) copy-start(f32[24,64]{1,0:T(8,128)} %copy-done.35) | copy-start | bytes 18436
  813.5 446.4 %reduce-scatter.21.cloned.1.call-start = ((), (), s32[]{:S(2)}) async-start(), calls=%async_computation.14 | async-start | bytes 589824 | tf_op jit(solution)/shard_map/reduce_scatter | solution.py:150
  814.2 483.4 %reduce-scatter.19.cloned.1.call-start = ((), (), s32[]{:S(2)}) async-start(), calls=%async_computation.13 | async-start | bytes 589824 | tf_op jit(solution)/shard_map/reduce_scatter | solution.py:149
  828.0 469.6 %copy-start.1 = (bf16[1024,1024]{1,0:T(8,128)(2,1)S(1)}, bf16[1024,1024]{1,0:T(8,128)(2,1)}, u32[]{:S(2)}) copy-start(bf16[1024,1024]{1,0:T(8,128)(2,1)} %param.19) | copy-start | bytes 6291460
  (8 other events, 20.6 us)
Sparse Core Ops, SparseCore 0:
  65.7 123.7 all-reduce.3
  233.7 221.8 all-reduce.5
  494.0 59.2 reduce-scatter.14
  555.5 211.7 reduce-scatter.16
  770.5 52.0 reduce-scatter.28
  824.8 135.7 reduce-scatter.30
  962.8 132.6 reduce-scatter.32
  1099.4 47.1 reduce-scatter.26
  1150.3 34.1 reduce-scatter.24
  1188.0 34.1 reduce-scatter.22
  1225.8 34.1 reduce-scatter.20
  1263.5 34.1 reduce-scatter.18
where the time goes:
time: 1310 us; the launch traced here: 1300 us
  waiting for transfers between devices  1030 us (79%)
  other arithmetic  112 us (9%)
  matrix products  107 us (8%)
  local copies, waits for them, and re-layouts  34.5 us (3%)
  between operations  15.6 us (1%)
    unnamed x14, waiting for transfers between devices  261 us
    psum x1, waiting for transfers between devices, body(): lax.psum(mlp_part.astype(jnp.bfloat16), 'head').astype(jnp.float32)  222 us
    reduce_scatter x1, waiting for transfers between devices, body(): lax.psum_scatter(media_part.astype(jnp.bfloat16), 'head', scatter_dimensi...  209 us
    psum x1, waiting for transfers between devices, body(): lax.psum(attn_part.astype(jnp.bfloat16), 'head').astype(jnp.float32)  124 us
    reduce_scatter x1, waiting for transfers between devices, body(): lax.psum_scatter(grad_up, 'img', scatter_dimension=0, tiled=True)  49.8 us
    reduce_scatter x1, waiting for transfers between devices, body(): lax.psum_scatter(grad_wout, 'img', scatter_dimension=0, tiled=True)  37.8 us
    reduce_scatter x1, waiting for transfers between devices, body(): lax.psum_scatter(grad_wk, 'img', scatter_dimension=0, tiled=True)  37.8 us
    reduce_scatter x1, waiting for transfers between devices, body(): lax.psum_scatter(grad_wq, 'img', scatter_dimension=0, tiled=True)  37.7 us
  transfers between devices with their start and end apart: 12, of which 12 were waited for; matrix products, arithmetic and copies ran while one was open for 9% of the time, Pallas kernels for 0%

commit v1 on v0

--- a/solution.py
+++ b/solution.py
@@ -88,7 +88,8 @@
     hidden_low = hidden.astype(jnp.bfloat16)
     mlp_part = jnp.einsum("ilf,df->ild", hidden_low, w_down, preferred_element_type=jnp.float32)
     latents_out = (
-        residual + lax.psum(mlp_part.astype(jnp.bfloat16), "head").astype(jnp.float32)
+        residual
+        + jnp.sum(lax.all_gather(mlp_part.astype(jnp.bfloat16), "head"), axis=0).astype(jnp.float32)
     ).astype(jnp.bfloat16)
     upstream = cotangent.astype(jnp.float32)
     grad_down = jnp.einsum("ild,ilf->df", cotangent, hidden_low, preferred_element_type=jnp.float32)

time: 1310 us -> 1420 us (1.084)
  waiting for transfers between devices: 1030 us -> 1130 us
  other arithmetic: 112 us -> 127 us
    all_gather x0 -> x1, waiting for transfers between devices: none -> 207 us  [body(): lax.all_gather(mlp_part.astype(jnp.bfloat16), 'head')]
    psum x1, waiting for transfers between devices: 222 us -> 112 us  [body(): lax.psum(grad_ffn_part.astype(jnp.bfloat16), 'head').astype(jnp.float32)]
    unnamed x14 -> x15, waiting for transfers between devices: 261 us -> 260 us
  transfers between devices with their start and end apart: 12 -> 13, of which waited for: 12 -> 13; matrix products, arithmetic and copies ran while one was open for 9% -> 9% of each run, Pallas kernels for 0% -> 0%
where the time goes in v1:
time: 1420 us
  waiting for transfers between devices  1130 us (80%)
  other arithmetic  127 us (9%)
  matrix products  108 us (8%)
  local copies, waits for them, and re-layouts  35.9 us (3%)
  between operations  15 us (1%)
    unnamed x15, waiting for transfers between devices  260 us
    reduce_scatter x1, waiting for transfers between devices, body(): lax.psum_scatter(media_part.astype(jnp.bfloat16), 'head', scatter_dimensi...  209 us
    all_gather x1, waiting for transfers between devices, body(): lax.all_gather(mlp_part.astype(jnp.bfloat16), 'head')  207 us
    psum x1, waiting for transfers between devices, body(): lax.psum(attn_part.astype(jnp.bfloat16), 'head').astype(jnp.float32)  123 us
    psum x1, waiting for transfers between devices, body(): lax.psum(grad_ffn_part.astype(jnp.bfloat16), 'head').astype(jnp.float32)  112 us
    reduce_scatter x1, waiting for transfers between devices, body(): lax.psum_scatter(grad_up, 'img', scatter_dimension=0, tiled=True)  50.1 us
    reduce_scatter x1, waiting for transfers between devices, body(): lax.psum_scatter(grad_wv, 'img', scatter_dimension=0, tiled=True)  37.8 us
    reduce_scatter x1, waiting for transfers between devices, body(): lax.psum_scatter(grad_wq, 'img', scatter_dimension=0, tiled=True)  37.8 us
  transfers between devices with their start and end apart: 13, of which 13 were waited for; matrix products, arithmetic and copies ran while one was open for 9% of the time, Pallas kernels for 0%

profile of v1, /device:TPU:0, one launch (start us, length us, event | category | flops | bytes accessed | tf_op | source)
XLA Modules:
  0.0 1418.1 jit_solution(12312669485396473193)
XLA Ops:
  7.8 2.4 convert_reduce_fusion.5
  10.2 2.9 multiply_reduce_fusion.3
  13.8 6.3 convert_reduce_fusion
  20.2 8.4 multiply_reduce_fusion
  29.3 2.2 fusion.41
  33.1 8.5 fusion.23
  42.7 2.2 pad_maximum_fusion.3
  45.0 4.1 copy.55
  49.1 4.1 copy.56
  53.3 5.5 fusion.74
  58.7 4.1 convolution_convert_fusion.6
  62.9 2.7 convolution_convert_fusion.3
  66.2 123.3 %all-reduce.3.cloned.1.call-done = bf16[24,64,1024]{2,1,0:T(8,128)(2,1)} async-done(((bf16[24,64,1024]{2,1,0:T(8,128)(2,1)}), bf16[24,64,1024]{2,1,0:T(8,128)(2,1)}) %all-reduce.3.cloned.1.call-update) | async-done | bytes 3145744 | tf_op jit(solution)/shard_map/psum | solution.py:84
  189.5 3.9 fusion.18
  195.6 5.7 convert_reduce_fusion.4
  201.3 14.8 %multiply_convert_fusion = (bf16[24,64,1024]{2,1,0:T(8,128)(2,1)}, f32[24,64,1024]{2,1,0:T(8,128)S(1)}) fusion(f32[24,64,1024]{2,1,0:T(8,128)S(1)} %get-tuple-element.84, u32[64,1024]{1,0:T(8,128)S(1)} %get-tuple-element.55, u32[64,1024]{1,0:T(8,128)S(1)} %get-tuple-element.54), kind=kLoop, calls=%fused_computation.35 | loop fusion | flops 106954752 | bytes 16252928 | tf_op jit(solution)/shard_map/convert_element_type | solution.py:88
  216.1 5.2 add_convert_fusion.4
  221.3 1.7 copy-done.53
  223.0 4.8 convolution_convert_fusion.1
  227.9 7.7 convolution_convert_fusion.2
  235.7 112.4 %all-reduce.5.cloned.1.call-done = bf16[24,64,1024]{2,1,0:T(8,128)(2,1)} async-done(((bf16[24,64,1024]{2,1,0:T(8,128)(2,1)}), bf16[24,64,1024]{2,1,0:T(8,128)(2,1)}) %all-reduce.5.cloned.1.call-update) | async-done | bytes 3145744 | tf_op jit(solution)/shard_map/psum | solution.py:100
  348.1 5.4 convert_reduce_fusion.2
  353.5 6.2 fusion.10
  359.8 207.1 %all-gather.3.cloned.1.call-done = bf16[96,64,1024]{2,1,0:T(8,128)(2,1)} async-done(((bf16[24,64,1024]{2,1,0:T(8,128)(2,1)}), bf16[96,64,1024]{2,1,0:T(8,128)(2,1)}) %all-gather.3.cloned.1.call-update) | async-done | bytes 12582928 | tf_op jit(solution)/shard_map/all_gather | solution.py:92
  566.9 10.6 reduce_sum.237
  577.4 8.5 add_add_fusion.2
  586.0 2.7 copy-done.4
  590.0 3.3 convolution_convert_fusion.5
  594.4 2.0 multiply_reduce_fusion.4
  599.0 2.2 multiply_convert_fusion.1
  603.6 4.7 convolution_convert_fusion.4
  608.4 1.6 slice.94
  610.0 2.7 slice.93
  612.7 1.6 copy.80
  614.3 1.9 copy.79
  616.2 8.5 convolution_convert_fusion
  624.9 8.4 convolution_bitcast_fusion
  633.3 5.3 convert_element_type.107
  638.6 14.4 %convert_element_type.108 = f32[24,256,1024]{2,1,0:T(8,128)} convert(bf16[24,256,1024]{2,1,0:T(8,128)(2,1)} %param.13) | non-fusion elementwise | flops 6291456 | bytes 37748736 | tf_op jit(solution)/shard_map/convert_element_type | solution.py:48
  653.0 1.6 dynamic-slice_reduce_fusion.1
  654.6 3.1 dynamic-slice_reduce_fusion
  657.8 9.3 reduce-scatter.15.cloned.1.call-done
  667.1 2.3 multiply_reduce_fusion.5
  669.4 2.5 fusion.36
  671.9 209.2 %reduce-scatter.17.cloned.1.call-done = bf16[24,64,1024]{2,1,0:T(8,128)(2,1)} async-done(((bf16[24,256,1024]{2,1,0:T(8,128)(2,1)}), bf16[24,64,1024]{2,1,0:T(8,128)(2,1)}) %reduce-scatter.17.cloned.1.call-update) | async-done | bytes 3145744 | tf_op jit(solution)/shard_map/reduce_scatter | solution.py:167
  881.1 6.1 multiply_reduce_fusion.1
  887.2 5.8 fusion.11
  895.4 10.5 convolution_bitcast_fusion.1
  906.0 6.3 fusion.47
  912.4 9.4 fusion.43
  921.9 4.1 fusion.42
  927.8 8.6 reduce-scatter.29.cloned.1.call-done
  936.4 2.0 copy.69
  938.5 3.3 add_convert_fusion.12
  941.9 6.1 add_convert_fusion.3
  948.0 126.6 %reduce-scatter.31.cloned.1.call-done = f32[32,3]{1,0:T(8,128)} async-done(((f32[1024,3]{1,0:T(8,128)}), f32[32,3]{1,0:T(8,128)}) %reduce-scatter.31.cloned.1.call-update) | async-done | bytes 400
  1074.6 1.4 copy.74
  1075.9 133.0 %reduce-scatter.33.cloned.1.call-done = f32[32,3]{1,0:T(8,128)} async-done(((f32[1024,3]{1,0:T(8,128)}), f32[32,3]{1,0:T(8,128)}) %reduce-scatter.33.cloned.1.call-update) | async-done | bytes 400
  1208.9 1.4 copy.76
  1210.3 50.1 %reduce-scatter.27.cloned.1.call-done = f32[128,1024]{1,0:T(8,128)} async-done(((f32[1024,1024]{1,0:T(8,128)}), f32[128,1024]{1,0:T(8,128)}) %reduce-scatter.27.cloned.1.call-update) | async-done | bytes 524304 | tf_op jit(solution)/shard_map/reduce_scatter | solution.py:154
  1260.4 37.6 %reduce-scatter.25.cloned.1.call-done = f32[128,128]{1,0:T(8,128)} async-done(((f32[1024,128]{1,0:T(8,128)}), f32[128,128]{1,0:T(8,128)}) %reduce-scatter.25.cloned.1.call-update) | async-done | bytes 65552 | tf_op jit(solution)/shard_map/reduce_scatter | solution.py:153
  1298.0 37.8 %reduce-scatter.23.cloned.1.call-done = f32[128,128]{1,0:T(8,128)} async-done(((f32[1024,128]{1,0:T(8,128)}), f32[128,128]{1,0:T(8,128)}) %reduce-scatter.23.cloned.1.call-update) | async-done | bytes 65552 | tf_op jit(solution)/shard_map/reduce_scatter | solution.py:152
  1335.9 37.7 %reduce-scatter.21.cloned.1.call-done = f32[128,128]{1,0:T(8,128)} async-done(((f32[1024,128]{1,0:T(8,128)}), f32[128,128]{1,0:T(8,128)}) %reduce-scatter.21.cloned.1.call-update) | async-done | bytes 65552 | tf_op jit(solution)/shard_map/reduce_scatter | solution.py:151
  1373.5 37.8 %reduce-scatter.19.cloned.1.call-done = f32[128,128]{1,0:T(8,128)} async-done(((f32[1024,128]{1,0:T(8,128)}), f32[128,128]{1,0:T(8,128)}) %reduce-scatter.19.cloned.1.call-update) | async-done | bytes 65552 | tf_op jit(solution)/shard_map/reduce_scatter | solution.py:150
  (175 shorter events, 19.6 us)
Async XLA Ops:
  7.2 188.4 %copy-start = (bf16[1024,1024]{1,0:T(8,128)(2,1)S(1)}, bf16[1024,1024]{1,0:T(8,128)(2,1)}, u32[]{:S(2)}) copy-start(bf16[1024,1024]{1,0:T(8,128)(2,1)} %param.19) | copy-start | bytes 6291460
  7.2 5.9 copy-start.43
  7.2 6.0 copy-start.44
  7.2 182.3 %all-reduce.3.cloned.1.call-start = ((), (), s32[]{:S(2)}) async-start(), calls=%async_computation.10 | async-start | bytes 6291456 | tf_op jit(solution)/shard_map/psum | solution.py:84
  10.2 19.0 %copy-start.38 = (f32[24,64]{1,0:T(8,128)}, f32[24,64]{1,0:T(8,128)S(1)}, u32[]{:S(2)}) copy-start(f32[24,64]{1,0:T(8,128)S(1)} %broadcast_multiply_fusion.4) | copy-start | bytes 18436
  13.1 16.1 %copy-start.42 = (f32[24,64]{1,0:T(8,128)}, f32[24,64]{1,0:T(8,128)S(1)}, u32[]{:S(2)}) copy-start(f32[24,64]{1,0:T(8,128)S(1)} %add_rsqrt_fusion.1) | copy-start | bytes 18436
  13.2 16.0 %copy-start.36 = (f32[1,1024]{1,0:T(1,128)}, f32[1,1024]{1,0:T(1,128)S(1)}, u32[]{:S(2)}) copy-start(f32[1,1024]{1,0:T(1,128)S(1)} %get-tuple-element.74) | copy-start | bytes 12292
  13.2 564.2 %copy-start.34 = (f32[1,1024]{1,0:T(1,128)}, f32[1,1024]{1,0:T(1,128)S(1)}, u32[]{:S(2)}) copy-start(f32[1,1024]{1,0:T(1,128)S(1)} %get-tuple-element.72) | copy-start | bytes 12292
  13.8 15.4 %copy-start.45 = (f32[1,1024]{1,0:T(1,128)}, f32[1,1024]{1,0:T(1,128)S(1)}, u32[]{:S(2)}) copy-start(f32[1,1024]{1,0:T(1,128)S(1)} %get-tuple-element.77) | copy-start | bytes 12292
  20.1 8.5 copy-start.32
  20.1 9.1 copy-start.2
  20.1 9.1 copy-start.24
  20.1 9.1 copy-start.26
  20.2 9.1 copy-start.52
  33.0 20.2 %copy-start.13 = (bf16[24,64,128]{1,2,0:T(8,128)(2,1)}, bf16[24,64,128]{1,2,0:T(8,128)(2,1)S(1)}, u32[]{:S(2)}) copy-start(bf16[24,64,128]{1,2,0:T(8,128)(2,1)S(1)} %copy.81) | copy-start | bytes 1179652
  45.0 8.2 copy-start.49
  45.0 8.2 copy-start.50
  58.7 4.1 copy-start.19
  65.6 130.0 %copy-start.48 = (f32[1,1024]{1,0:T(1,128)S(1)}, f32[1,1024]{1,0:T(1,128)}, u32[]{:S(2)}) copy-start(f32[1,1024]{1,0:T(1,128)} %get-tuple-element.75) | copy-start | bytes 12292
  65.6 282.5 %all-reduce.5.cloned.1.call-start = ((), (), s32[]{:S(2)}) async-start(), calls=%async_computation.11 | async-start | bytes 6291456 | tf_op jit(solution)/shard_map/psum | solution.py:100
  189.5 3.9 copy-start.3
  189.5 4.7 copy-start.5
  201.3 14.9 %copy-start.12 = (bf16[24,64,1024]{2,1,0:T(8,128)(2,1)S(1)}, bf16[24,64,1024]{2,1,0:T(8,128)(2,1)}, u32[]{:S(2)}) copy-start(bf16[24,64,1024]{2,1,0:T(8,128)(2,1)} %param.23) | copy-start | bytes 9437188
  201.3 14.8 %copy-start.51 = (bf16[1024,1024]{1,0:T(8,128)(2,1)S(1)}, bf16[1024,1024]{1,0:T(8,128)(2,1)}, u32[]{:S(2)}) copy-start(bf16[1024,1024]{1,0:T(8,128)(2,1)} %param.20) | copy-start | bytes 6291460
  227.8 339.0 %all-gather.3.cloned.1.call-start = ((), (), s32[]{:S(2)}) async-start(), calls=%async_computation.20 | async-start | bytes 15728640 | tf_op jit(solution)/shard_map/all_gather | solution.py:92
  235.6 431.5 %reduce-scatter.15.cloned.1.call-start = ((), (), s32[]{:S(2)}) async-start(), calls=%async_computation.12 | async-start | bytes 3932160 | tf_op jit(solution)/shard_map/reduce_scatter | solution.py:170
  348.1 5.5 copy-start.7
  577.4 11.2 copy-start.20
  586.0 2.7 copy-start.4
  588.6 4.8 slice-start
  590.0 3.6 slice-start.1
  590.0 4.4 copy-start.16
  594.4 6.8 copy-start.15
  601.9 6.4 copy-start.21
  603.6 4.7 copy-start.23
  608.3 272.8 %reduce-scatter.17.cloned.1.call-start = ((), (), s32[]{:S(2)}) async-start(), calls=%async_computation.13 | async-start | bytes 15728640 | tf_op jit(solution)/shard_map/reduce_scatter | solution.py:167
  608.4 7.8 copy-start.25
  608.4 7.8 copy-start.27
  616.2 8.6 copy-start.11
  624.8 311.6 %reduce-scatter.29.cloned.1.call-start = ((), (), s32[]{:S(2)}) async-start(), calls=%async_computation.19 | async-start | bytes 4718592 | tf_op jit(solution)/shard_map/reduce_scatter | solution.py:155
  633.2 441.3 %reduce-scatter.31.cloned.1.call-start = ((), (), s32[]{:S(2)}) async-start(), calls=%async_computation.21 | async-start | bytes 540672
  653.0 14.1 copy-start.37
  881.1 6.1 copy-start.6
  887.2 8.2 copy-start.35
  887.2 18.7 %copy-start.28 = (f32[24,64]{1,0:T(8,128)}, f32[24,64]{1,0:T(8,128)S(1)}, u32[]{:S(2)}) copy-start(f32[24,64]{1,0:T(8,128)S(1)} %get-tuple-element.78) | copy-start | bytes 18436
  887.2 18.7 %copy-start.30 = (f32[24,64]{1,0:T(8,128)}, f32[24,64]{1,0:T(8,128)S(1)}, u32[]{:S(2)}) copy-start(f32[24,64]{1,0:T(8,128)S(1)} %get-tuple-element.79) | copy-start | bytes 18436
  894.2 314.8 %reduce-scatter.33.cloned.1.call-start = ((), (), s32[]{:S(2)}) async-start(), calls=%async_computation.22 | async-start | bytes 540672
  895.3 365.1 %reduce-scatter.27.cloned.1.call-start = ((), (), s32[]{:S(2)}) async-start(), calls=%async_computation.18 | async-start | bytes 4718592 | tf_op jit(solution)/shard_map/reduce_scatter | solution.py:154
  905.9 6.4 copy-start.10
  905.9 6.4 copy-start.33
  905.9 6.4 copy-start.41
  906.0 6.4 copy-start.47
  906.0 392.1 %reduce-scatter.25.cloned.1.call-start = ((), (), s32[]{:S(2)}) async-start(), calls=%async_computation.17 | async-start | bytes 589824 | tf_op jit(solution)/shard_map/reduce_scatter | solution.py:153
  912.3 9.5 copy-start.22
  912.4 9.5 copy-start.39
  912.4 9.5 copy-start.46
  921.8 414.1 %reduce-scatter.23.cloned.1.call-start = ((), (), s32[]{:S(2)}) async-start(), calls=%async_computation.16 | async-start | bytes 589824 | tf_op jit(solution)/shard_map/reduce_scatter | solution.py:152
  925.9 12.6 copy-start.9
  925.9 15.9 %copy-start.40 = (f32[24,64]{1,0:T(8,128)S(1)}, f32[24,64]{1,0:T(8,128)}, u32[]{:S(2)}) copy-start(f32[24,64]{1,0:T(8,128)} %get-tuple-element.45) | copy-start | bytes 18436
  925.9 15.9 %copy-start.29 = (f32[24,64]{1,0:T(8,128)S(1)}, f32[24,64]{1,0:T(8,128)}, u32[]{:S(2)}) copy-start(f32[24,64]{1,0:T(8,128)} %copy-done.28) | copy-start | bytes 18436
  925.9 15.9 %copy-start.31 = (f32[24,64]{1,0:T(8,128)S(1)}, f32[24,64]{1,0:T(8,128)}, u32[]{:S(2)}) copy-start(f32[24,64]{1,0:T(8,128)} %copy-done.30) | copy-start | bytes 18436
  927.2 446.3 %reduce-scatter.21.cloned.1.call-start = ((), (), s32[]{:S(2)}) async-start(), calls=%async_computation.15 | async-start | bytes 589824 | tf_op jit(solution)/shard_map/reduce_scatter | solution.py:151
  927.8 483.6 %reduce-scatter.19.cloned.1.call-start = ((), (), s32[]{:S(2)}) async-start(), calls=%async_computation.14 | async-start | bytes 589824 | tf_op jit(solution)/shard_map/reduce_scatter | solution.py:150
  941.8 469.5 %copy-start.1 = (bf16[1024,1024]{1,0:T(8,128)(2,1)S(1)}, bf16[1024,1024]{1,0:T(8,128)(2,1)}, u32[]{:S(2)}) copy-start(bf16[1024,1024]{1,0:T(8,128)(2,1)} %param.19) | copy-start | bytes 6291460
  (5 other events, 8.1 us)
Sparse Core Ops, SparseCore 0:
  65.7 123.7 all-reduce.2
  228.0 120.0 all-reduce.4
  349.6 217.1 all-gather.2
  608.4 58.5 reduce-scatter.14
  669.3 211.7 reduce-scatter.16
  884.3 52.0 reduce-scatter.28
  938.7 135.8 reduce-scatter.30
  1076.8 132.0 reduce-scatter.32
  1212.9 47.4 reduce-scatter.26
  1263.9 34.0 reduce-scatter.24
  1301.7 34.1 reduce-scatter.22
  1339.4 34.1 reduce-scatter.20
  1377.2 34.1 reduce-scatter.18
